TPU v7x, 128 devices: a whole 4x4x4 slice. The times are simulated.
128 devices in a mesh: orow: 16 (over z, x), ocol: 8 (over y, core).
Axes of the slice: x: 4, y: 4, z: 4, core: 2. Of those that a mesh axis runs over, the one named last changes fastest.
Arguments:
- integrals: bfloat16 [2304, 32, 384], P('ocol', 'orow'), may hold values from -0.29882812 to 0.29882812
- occ_count: int32 [16], replicated, may hold values from 1 to 2
- occ_energy: float32 [32], replicated, may hold values from -2 to -0.5
- vir_energy: float32 [384], replicated, may hold values from 0.3 to 2.5
- task_iblock: int32 [64, 1], replicated, may hold values from 0 to 15; in each aligned block of 64 rows (0 to 63, 64 to 127, ...) at most 8 rows name the same one
- task_jblock: int32 [64], replicated, may hold values from 0 to 15
Outputs:
- gamma_out: float32 [2304, 32, 384], P('ocol', 'orow')
- density: float32 [384, 384], replicated
Inputs may be any that keep to these rules, and one draw needn't show every extreme that they name: `task_iblock`: no first block is named by more than 8 tasks, and some first block by exactly 8.
All inputs are finite; a program needn't handle non-finite values.
Results may differ from a plain program's by a relative error of at most 0.0019.
Values may be sent and summed in bfloat16 or wider, within the bound.
No kernel may reach another device: no remote copies, remote signals or barrier semaphores. Data moves between devices by JAX's collectives and lax.ppermute only.
A program may use at most 128 MiB of HBM per device.

v0:
```python
import jax
import jax.numpy as jnp
from jax import lax
from jax.sharding import Mesh
from jax.sharding import PartitionSpec as P

OROW = ("orow_0", "orow_1")
OCOL = ("ocol_0", "ocol_1")
OROW_OCOL = ("orow_0", "orow_1", "ocol_0", "ocol_1")


def rows_for(lines, length):
    spare = -lines.shape[0] % length
    if not spare:
        return lines
    return jnp.concatenate([lines, jnp.zeros((spare, *lines.shape[1:]), lines.dtype)])


def sum_in_order(pieces, axes, turns):
    lengths = [lax.axis_size(a) for a in axes]
    pieces = pieces.reshape(*lengths, *pieces.shape[1:])
    pieces = pieces.transpose(*turns, *range(len(axes), pieces.ndim))
    pieces = pieces.reshape(-1, *pieces.shape[len(axes) :])
    for k in turns:
        pieces = lax.psum_scatter(pieces, axes[k], scatter_dimension=0, tiled=True)
    return pieces[0]


def gather_in_order(x, axes, turns):
    pieces = x
    for k in turns:
        pieces = lax.all_gather(pieces, axes[k])
    done = turns[::-1]
    back = [done.index(k) for k in range(len(axes))]
    pieces = pieces.transpose(*back, *range(len(axes), pieces.ndim))
    return pieces.reshape(-1, *x.shape)


def total_of(x, axes, turns):
    length, lines = (lax.axis_size(axes), x.reshape(-1, *x.shape[1:][-1:]))
    pieces = rows_for(lines, length).reshape(length, -1, *lines.shape[1:])
    own = sum_in_order(pieces, axes, turns)
    whole = gather_in_order(own, axes, turns[::-1]).reshape(-1, *lines.shape[1:])
    return whole[: len(lines)].reshape(x.shape)


def make_amplitudes(k_total, i_energy, j_energy, vir_energy, usable):
    slots = k_total.shape[0]
    orbitals = i_energy.shape[1]
    virtuals = vir_energy.shape[0]
    k_grid = k_total.reshape(slots, orbitals, virtuals, orbitals, virtuals)
    denominator = (
        i_energy[:, :, None, None, None]
        + j_energy[:, None, None, :, None]
        - vir_energy[None, None, :, None, None]
        - vir_energy[None, None, None, None, :]
    )
    values = (2.0 * k_grid - jnp.swapaxes(k_grid, 2, 4)) / denominator
    values = values * usable[:, None, None, None, None]
    return values.astype(jnp.bfloat16).reshape(slots, orbitals * virtuals, orbitals * virtuals)


def local(integrals, occ_count, occ_energy, vir_energy, task_iblock, task_jblock):
    aux_local = integrals.shape[0]
    orbitals = integrals.shape[1]
    virtuals = integrals.shape[2]
    span = orbitals * virtuals
    block_total = lax.axis_size(OROW)
    col_total = lax.axis_size(OCOL)
    my_row = lax.axis_index(OROW)
    my_col = lax.axis_index(OCOL)
    active = jnp.arange(orbitals) < occ_count[my_row]
    masked = integrals * active.astype(jnp.bfloat16)[None, :, None]
    gathered = lax.all_gather(masked, OROW, axis=1, tiled=True)
    flat_blocks = gathered.reshape(aux_local, block_total, span)
    first_list = task_iblock[:, 0]
    task_total = first_list.shape[0]
    per_row = task_total // block_total
    task_ids = my_row * per_row + jnp.arange(per_row)
    i_block = first_list[task_ids]
    j_block = task_jblock[task_ids]
    usable = jnp.ones((per_row,), jnp.float32)
    energy_grid = occ_energy.reshape(block_total, orbitals)
    i_rows = jnp.take(flat_blocks, i_block, axis=1)
    j_rows = jnp.take(flat_blocks, j_block, axis=1)
    k_partial = jnp.einsum("psx,psy->sxy", i_rows, j_rows, preferred_element_type=jnp.float32)
    slots = k_partial.shape[0]
    i_energy = energy_grid[i_block]
    j_energy = energy_grid[j_block]
    k_total = lax.psum(k_partial, OCOL)
    amplitudes = make_amplitudes(k_total, i_energy, j_energy, vir_energy, usable)
    gamma_i = jnp.einsum("sxy,psy->psx", amplitudes, j_rows, preferred_element_type=jnp.float32)
    gamma_j = jnp.einsum("sxy,psx->psy", amplitudes, i_rows, preferred_element_type=jnp.float32)
    slice_width = span // col_total
    amp_grid = amplitudes.reshape(slots, orbitals, virtuals, span)
    column_part = lax.dynamic_slice_in_dim(amp_grid, my_col * slice_width, slice_width, 3)
    dens_part = jnp.einsum(
        "siaw,sibw->ab", column_part, column_part, preferred_element_type=jnp.float32
    )
    block_ids = jnp.arange(block_total)
    i_onehot = (i_block[:, None] == block_ids[None, :]).astype(jnp.float32)
    j_onehot = (j_block[:, None] == block_ids[None, :]).astype(jnp.float32)
    buffer = jnp.einsum(
        "sk,psx->pkx", i_onehot, gamma_i, precision=lax.Precision.HIGHEST
    ) + jnp.einsum("sk,psx->pkx", j_onehot, gamma_j, precision=lax.Precision.HIGHEST)
    owned = lax.psum_scatter(buffer, OROW, scatter_dimension=1, tiled=True)
    gamma_out = owned.reshape(aux_local, orbitals, virtuals)
    density = total_of(dens_part, OROW_OCOL, (0, 1, 2, 3)) / task_total
    return (gamma_out, density)


def solution(mesh):
    finer = Mesh(mesh.devices.reshape(4, 4, 4, 2), ("orow_0", "orow_1", "ocol_0", "ocol_1"))
    placed = (P(OCOL, OROW, None), P(), P(), P(), P(), P())
    return jax.shard_map(
        local, mesh=finer, in_specs=placed, out_specs=(P(OCOL, OROW, None), P()), check_vma=False
    )
```

profile of v0, /device:TPU:1, one launch (start us, length us, event | category | flops | bytes accessed | tf_op | source)
XLA Modules:
  0.0 520.0 jit_solution(48696897312067520)
XLA Ops:
  13.1 66.1 %all-gather.5.cloned.1.call-done = bf16[288,32,384]{2,0,1:T(8,128)(2,1)} async-done(((bf16[288,2,384]{2,0,1:T(8,128)(2,1)}), bf16[288,32,384]{2,0,1:T(8,128)(2,1)}) %all-gather.5.cloned.1.call-update) | async-done | bytes 7077904 | tf_op jit(solution)/shard_map/all_gather | solution.py:74
  79.2 8.5 %copy.47 = bf16[288,32,384]{2,1,0:T(8,128)(2,1)} copy(bf16[288,32,384]{2,0,1:T(8,128)(2,1)} %all-gather.5.cloned.1.call-done) | data formatting | bytes 14155776 | tf_op jit(solution)/shard_map/all_gather | solution.py:74
  87.8 11.3 %reshape.91 = bf16[288,16,768]{2,1,0:T(8,128)(2,1)} reshape(bf16[288,32,384]{2,1,0:T(8,128)(2,1)} %copy.47) | data formatting | bytes 14155776 | tf_op jit(solution)/shard_map/reshape | solution.py:75
  99.1 8.3 %copy.48 = bf16[288,16,768]{2,0,1:T(8,128)(2,1)} copy(bf16[288,16,768]{2,1,0:T(8,128)(2,1)} %reshape.91) | data formatting | bytes 14155776 | tf_op jit(solution)/shard_map/reshape | solution.py:75
  114.8 5.2 fusion.6
  120.0 12.5 %reshape.92 = f32[4,2,384,2,384]{4,3,2,1,0:T(2,128)} reshape(f32[4,768,768]{2,1,0:T(8,128)} %fusion.6) | data formatting | bytes 18874368 | tf_op jit(solution)/shard_map/reshape | solution.py:51
  132.5 14.8 %copy.50 = f32[4,2,384,2,384]{2,4,3,1,0:T(8,128)} copy(f32[4,2,384,2,384]{4,3,2,1,0:T(2,128)} %reshape.92) | data formatting | bytes 18874368 | tf_op jit(solution)/shard_map/reshape | solution.py:51
  157.6 103.2 %all-reduce.9.cloned.1.call-done = f32[4,2,384,2,384]{2,4,3,1,0:T(8,128)} async-done(((f32[4,2,384,2,384]{2,4,3,1,0:T(8,128)}), f32[4,2,384,2,384]{2,4,3,1,0:T(8,128)}) %all-reduce.9.cloned.1.call-update) | async-done | bytes 9437200 | tf_op jit(solution)/shard_map/psum | solution.py:90
  260.8 9.6 %copy.51 = f32[4,2,384,2,384]{4,2,3,1,0:T(8,128)} copy(f32[4,2,384,2,384]{2,4,3,1,0:T(8,128)} %all-reduce.9.cloned.1.call-done) | data formatting | bytes 18874368 | tf_op jit(solution)/shard_map/psum | solution.py:90
  270.4 9.6 %fusion.1 = bf16[4,2,384,2,384]{4,2,3,1,0:T(8,128)(2,1)} fusion(f32[4,2,384,2,384]{2,4,3,1,0:T(8,128)} %all-reduce.9.cloned.1.call-done, f32[4,2,384,2,384]{4,2,3,1,0:T(8,128)} %copy.51, f32[384]{0:T(512)S(1)} %copy-done.2, f32[4,2,384,2]{2,3,1,0:T(2,128)} %broadcast_subtract_fusion), kind=kLoop, calls=%fused_computation.9 | loop fusion | flops 11796480 | bytes 23619072 | tf_op jit(solution)/shard_map/convert_element_type | solution.py:60
  280.0 6.7 %copy.63 = bf16[4,2,384,2,384]{2,4,3,0,1:T(8,128)(2,1)} copy(bf16[4,2,384,2,384]{4,2,3,1,0:T(8,128)(2,1)} %fusion.1) | data formatting | bytes 9437184 | tf_op jit(solution)/shard_map/reshape;reshape | solution.py:95
  286.7 9.4 %copy.52 = bf16[4,2,384,2,384]{4,3,2,1,0:T(2,128)(2,1)} copy(bf16[4,2,384,2,384]{4,2,3,1,0:T(8,128)(2,1)} %fusion.1) | data formatting | bytes 9437184 | tf_op jit(solution)/shard_map/convert_element_type | solution.py:60
  296.1 11.4 %reshape.94 = bf16[4,768,768]{2,1,0:T(8,128)(2,1)} reshape(bf16[4,2,384,2,384]{4,3,2,1,0:T(2,128)(2,1)} %copy.52) | data formatting | bytes 9437184 | tf_op jit(solution)/shard_map/reshape | solution.py:60
  316.5 9.7 %fusion.3 = f32[288,768,16]{1,2,0:T(8,128)} fusion(f32[288,4,768]{2,0,1:T(8,128)S(1)} %convolution_bitcast_fusion.1, s32[4]{0:T(128)S(1)} %copy-done.4), kind=kOutput, calls=%fused_computation.11 | convolution fusion | flops 169869376 | bytes 17694736 | tf_op jit(solution)/shard_map/sk,psx->pkx/dot_general | solution.py:103
  329.5 25.9 %all-reduce.11.cloned.1.call-done = f32[128,3,384]{2,1,0:T(4,128)} async-done(((f32[128,3,384]{2,1,0:T(4,128)}), f32[128,3,384]{2,1,0:T(4,128)}) %all-reduce.11.cloned.1.call-update) | async-done | bytes 589840
  357.1 15.3 %add_bitcast_fusion = f32[288,16,768]{2,1,0:T(8,128)} fusion(f32[288,768,16]{1,2,0:T(8,128)} %fusion.3, f32[288,4,768]{2,0,1:T(8,128)} %convolution_bitcast_fusion, s32[4]{0:T(128)S(1)} %copy-done.6), kind=kOutput, calls=%fused_computation.6 | convolution fusion | flops 173408320 | bytes 31850512 | tf_op jit(solution)/shard_map/sk,psx->pkx/dot_general | solution.py:105
  372.4 18.3 %copy.55 = f32[288,16,768]{2,0,1:T(8,128)} copy(f32[288,16,768]{2,1,0:T(8,128)} %add_bitcast_fusion) | data formatting | bytes 28311552 | tf_op jit(solution)/shard_map/add | solution.py:103
  394.4 5.8 %all-reduce.13.cloned.1.call-done = f32[32,3,384]{2,1,0:T(4,128)} async-done(((f32[32,3,384]{2,1,0:T(4,128)}), f32[32,3,384]{2,1,0:T(4,128)}) %all-reduce.13.cloned.1.call-update) | async-done | bytes 147472
  401.0 14.0 %all-reduce.3 = f32[8,3,384]{2,1,0:T(4,128)S(1)} all-reduce(f32[8,3,384]{2,1,0:T(4,128)S(1)} %constant_dynamic-slice_fusion.1), channel_id=8, replica_groups=mesh['orow_0'=4,'orow_1'=4,'ocol_0'=4,'ocol_1'=2] {'ocol_0'}, use_global_device_ids=true, to_apply=%region_4.6.clone | all-reduce | flops 9216 | bytes 73728
  415.0 9.2 %all-reduce.4 = f32[2,3,384]{2,1,0:T(4,128)S(1)} all-reduce(f32[2,3,384]{2,1,0:T(4,128)S(1)} %constant_dynamic-slice_fusion), channel_id=9, replica_groups=mesh['orow_0'=4,'orow_1'=4,'ocol_0'=4,'ocol_1'=2] {'ocol_1'}, use_global_device_ids=true, to_apply=%region_5.7.clone | all-reduce | flops 2304 | bytes 18432
  426.7 10.1 %all-gather = f32[8,3,384]{2,1,0:T(4,128)S(1)} all-gather(f32[2,3,384]{2,1,0:T(4,128)S(1)} %all_gather.25), channel_id=2, replica_groups=mesh['orow_0'=4,'orow_1'=4,'ocol_0'=4,'ocol_1'=2] {'ocol_0'}, dimensions={0}, use_global_device_ids=true | all-gather | bytes 46080 | tf_op jit(solution)/shard_map/all_gather | solution.py:32
  436.9 11.4 %all-gather.1 = f32[16,2,3,384]{3,1,2,0:T(2,128)S(1)} all-gather(f32[4,2,3,384]{3,1,2,0:T(2,128)S(1)} %copy.58), channel_id=3, replica_groups=mesh['orow_0'=4,'orow_1'=4,'ocol_0'=4,'ocol_1'=2] {'orow_1'}, dimensions={0}, use_global_device_ids=true | all-gather | bytes 184320 | tf_op jit(solution)/shard_map/all_gather | solution.py:32
  448.3 14.9 %all-gather.2 = f32[16,4,2,3,384]{4,1,3,2,0:T(4,128)S(1)} all-gather(f32[4,4,2,3,384]{4,1,3,2,0:T(4,128)S(1)} %copy.59), channel_id=4, replica_groups=mesh['orow_0'=4,'orow_1'=4,'ocol_0'=4,'ocol_1'=2] {'orow_0'}, dimensions={0}, use_global_device_ids=true | all-gather | bytes 737280 | tf_op jit(solution)/shard_map/all_gather | solution.py:32
  464.7 46.0 %reduce-scatter.4.cloned.1.call-done = f32[288,1,768]{2,0,1:T(8,128)} async-done(((f32[288,16,768]{2,0,1:T(8,128)}), f32[288,1,768]{2,0,1:T(8,128)}) %reduce-scatter.4.cloned.1.call-update) | async-done | bytes 884752
  (77 shorter events, 46.6 us)
Async XLA Ops:
  7.2 4.0 copy-start
  7.2 72.1 %all-gather.5.cloned.1.call-start = ((), (), s32[]{:S(2)}) async-start(), calls=%async_computation.1 | async-start | bytes 7520256 | tf_op jit(solution)/shard_map/all_gather | solution.py:74
  11.0 249.8 %all-reduce.9.cloned.1.call-start = ((), (), s32[]{:S(2)}) async-start(), calls=%async_computation.2 | async-start | bytes 18874368 | tf_op jit(solution)/shard_map/psum | solution.py:90
  11.8 76.0 %copy-start.3 = (s32[4]{0:T(128)}, s32[4]{0:T(128)S(1)}, u32[]{:S(2)}) copy-start(s32[4]{0:T(128)S(1)} %gather_fusion.1) | copy-start | bytes 52
  13.1 74.7 %copy-start.5 = (s32[4]{0:T(128)}, s32[4]{0:T(128)S(1)}, u32[]{:S(2)}) copy-start(s32[4]{0:T(128)S(1)} %gather_fusion) | copy-start | bytes 52
  147.3 208.0 %all-reduce.11.cloned.1.call-start = ((), (), s32[]{:S(2)}) async-start(), calls=%async_computation.3 | async-start | bytes 1572864
  157.6 112.8 %copy-start.2 = (f32[384]{0:T(512)S(1)}, f32[384]{0:T(512)}, u32[]{:S(2)}) copy-start(f32[384]{0:T(512)} %param.11) | copy-start | bytes 4612
  312.3 4.2 copy-start.4
  312.3 87.9 %all-reduce.13.cloned.1.call-start = ((), (), s32[]{:S(2)}) async-start(), calls=%async_computation.4 | async-start | bytes 393216
  312.5 13.7 %slice-start = ((s8[4718592]{0:T(1024)(128)(4,1)}), s8[524288]{0:T(1024)(128)(4,1)S(1)}, s32[]{:S(2)}) async-start(s8[4718592]{0:T(1024)(128)(4,1)} %bitcast.58), calls=%async_computation.6 | async-start | bytes 1048576
  316.5 9.7 %slice-start.1 = ((s8[4718592]{0:T(1024)(128)(4,1)}), s8[4194304]{0:T(1024)(128)(4,1)S(1)}, s32[]{:S(2)}) async-start(s8[4718592]{0:T(1024)(128)(4,1)} %bitcast.58), calls=%async_computation.7 | async-start | bytes 8388608
  326.2 30.9 %copy-start.6 = (s32[4]{0:T(128)S(1)}, s32[4]{0:T(128)}, u32[]{:S(2)}) copy-start(s32[4]{0:T(128)} %copy-done.5) | copy-start | bytes 52
  357.0 153.6 %reduce-scatter.4.cloned.1.call-start = ((), (), s32[]{:S(2)}) async-start(), calls=%async_computation.5 | async-start | bytes 15040512
  390.7 0.7 copy-start.9
  390.7 1.2 copy-start.8
  390.7 1.9 copy-start.7
  391.3 121.9 %copy-start.1 = (s32[64,1]{0,1:T(1,128)S(1)}, s32[64,1]{0,1:T(1,128)}, u32[]{:S(2)}) copy-start(s32[64,1]{0,1:T(1,128)} %param.12) | copy-start | bytes 772
Sparse Core Ops, SparseCore 0:
  11.2 68.0 all-gather.4
  147.5 113.3 all-reduce.8
  312.4 42.9 all-reduce.10
  358.1 42.0 all-reduce.12
  403.6 107.0 reduce-scatter.3
where the time goes:
time: 529 us; the launch traced here: 520 us
  waiting for transfers between devices  247 us (47%)
  local copies, waits for them, and re-layouts  138 us (26%)
  blocking collectives  61.5 us (12%)
  matrix products  40 us (8%)
  other arithmetic  16.9 us (3%)
  between operations  16.2 us (3%)
    psum x1, waiting for transfers between devices, local(): k_total = lax.psum(k_partial, OCOL)  103 us
    unnamed x8, waiting for transfers between devices  77.7 us
    all_gather x1, waiting for transfers between devices, local(): gathered = lax.all_gather(masked, OROW, axis=1, tiled=True)  66.1 us
    all_gather x4, blocking collectives, gather_in_order(): pieces = lax.all_gather(pieces, axes[k])  38.2 us
    reshape x2, local copies, waits for them, and re-layouts, make_amplitudes(): k_grid = k_total.reshape(slots, orbitals, virtuals, orbitals, virtuals)  27.3 us
    unnamed x2, blocking collectives  23.3 us
    reshape x2, local copies, waits for them, and re-layouts, local(): flat_blocks = gathered.reshape(aux_local, block_total, span)  19.6 us
    add x1, local copies, waits for them, and re-layouts, local(): jnp.einsum('sk,psx->pkx', i_onehot, gamma_i, precision=lax.Precision.HIGH...  18.3 us
  transfers between devices with their start and end apart: 5, of which 5 were waited for; matrix products, arithmetic and copies ran while one was open for 13% of the time, Pallas kernels for 0%

commit v1 on v0

--- a/solution.py
+++ b/solution.py
@@ -87,7 +87,7 @@
     slots = k_partial.shape[0]
     i_energy = energy_grid[i_block]
     j_energy = energy_grid[j_block]
-    k_total = lax.psum(k_partial, OCOL)
+    k_total = jnp.sum(lax.all_gather(k_partial, OCOL), axis=0)
     amplitudes = make_amplitudes(k_total, i_energy, j_energy, vir_energy, usable)
     gamma_i = jnp.einsum("sxy,psy->psx", amplitudes, j_rows, preferred_element_type=jnp.float32)
     gamma_j = jnp.einsum("sxy,psx->psy", amplitudes, i_rows, preferred_element_type=jnp.float32)

time: 529 us -> 770 us (1.46)
  waiting for transfers between devices: 247 us -> 464 us
  other arithmetic: 16.9 us -> 45.5 us
  local copies, waits for them, and re-layouts: 138 us -> 127 us
    all_gather x0 -> x1, waiting for transfers between devices: none -> 324 us  [local(): k_total = jnp.sum(lax.all_gather(k_partial, OCOL), axis=0)]
    psum x1 -> x0, waiting for transfers between devices: 103 us -> none  [local(): k_total = lax.psum(k_partial, OCOL)]
    reduce_sum x0 -> x1, other arithmetic: none -> 28.2 us  [local(): k_total = jnp.sum(lax.all_gather(k_partial, OCOL), axis=0)]
    psum x1 -> x0, local copies, waits for them, and re-layouts: 9.6 us -> none  [local(): k_total = lax.psum(k_partial, OCOL)]
  transfers between devices with their start and end apart: 5 -> 5, of which waited for: 5 -> 5; matrix products, arithmetic and copies ran while one was open for 13% -> 9% of each run, Pallas kernels for 0% -> 0%
where the time goes in v1:
time: 770 us; the launch traced here: 762 us
  waiting for transfers between devices  464 us (60%)
  local copies, waits for them, and re-layouts  127 us (16%)
  blocking collectives  61.5 us (8%)
  matrix products  47 us (6%)
  other arithmetic  45.5 us (6%)
  between operations  16.1 us (2%)
    all_gather x1, waiting for transfers between devices, local(): k_total = jnp.sum(lax.all_gather(k_partial, OCOL), axis=0)  324 us
    unnamed x8, waiting for transfers between devices  74.1 us
    all_gather x1, waiting for transfers between devices, local(): gathered = lax.all_gather(masked, OROW, axis=1, tiled=True)  66.1 us
    all_gather x4, blocking collectives, gather_in_order(): pieces = lax.all_gather(pieces, axes[k])  38.2 us
    reduce_sum x1, other arithmetic, local(): k_total = jnp.sum(lax.all_gather(k_partial, OCOL), axis=0)  28.2 us
    reshape x2, local copies, waits for them, and re-layouts, make_amplitudes(): k_grid = k_total.reshape(slots, orbitals, virtuals, orbitals, virtuals)  27.3 us
    unnamed x2, blocking collectives  23.3 us
    reshape x2, local copies, waits for them, and re-layouts, local(): flat_blocks = gathered.reshape(aux_local, block_total, span)  19.6 us
  transfers between devices with their start and end apart: 5, of which 5 were waited for; matrix products, arithmetic and copies ran while one was open for 9% of the time, Pallas kernels for 0%

profile of v1, /device:TPU:1, one launch (start us, length us, event | category | flops | bytes accessed | tf_op | source)
XLA Modules:
  0.0 761.7 jit_solution(11132989784302936038)
XLA Ops:
  13.1 66.1 %all-gather.7.cloned.1.call-done = bf16[288,32,384]{2,0,1:T(8,128)(2,1)} async-done(((bf16[288,2,384]{2,0,1:T(8,128)(2,1)}), bf16[288,32,384]{2,0,1:T(8,128)(2,1)}) %all-gather.7.cloned.1.call-update) | async-done | bytes 7077904 | tf_op jit(solution)/shard_map/all_gather | solution.py:74
  79.2 8.5 %copy.48 = bf16[288,32,384]{2,1,0:T(8,128)(2,1)} copy(bf16[288,32,384]{2,0,1:T(8,128)(2,1)} %all-gather.7.cloned.1.call-done) | data formatting | bytes 14155776 | tf_op jit(solution)/shard_map/all_gather | solution.py:74
  87.8 11.3 %reshape.91 = bf16[288,16,768]{2,1,0:T(8,128)(2,1)} reshape(bf16[288,32,384]{2,1,0:T(8,128)(2,1)} %copy.48) | data formatting | bytes 14155776 | tf_op jit(solution)/shard_map/reshape | solution.py:75
  99.1 8.4 %copy.49 = bf16[288,16,768]{2,0,1:T(8,128)(2,1)} copy(bf16[288,16,768]{2,1,0:T(8,128)(2,1)} %reshape.91) | data formatting | bytes 14155776 | tf_op jit(solution)/shard_map/reshape | solution.py:75
  129.8 324.3 %all-gather.9.cloned.1.call-done = f32[32,768,768]{2,1,0:T(8,128)} async-done(((f32[4,768,768]{2,1,0:T(8,128)}), f32[32,768,768]{2,1,0:T(8,128)}) %all-gather.9.cloned.1.call-update) | async-done | bytes 75497488 | tf_op jit(solution)/shard_map/all_gather | solution.py:90
  454.1 28.2 %reduce_sum.9 = f32[4,768,768]{2,1,0:T(8,128)} reduce(f32[8,4,768,768]{3,2,1,0:T(8,128)} %bitcast.5, f32[]{:T(128)} %constant.16.clone.1), dimensions={0}, to_apply=%region_0.0 | reduce | flops 16515072 | bytes 84934656 | tf_op jit(solution)/shard_map/reduce_sum | solution.py:90
  482.3 12.5 %reshape.92 = f32[4,2,384,2,384]{4,3,2,1,0:T(2,128)} reshape(f32[4,768,768]{2,1,0:T(8,128)} %reduce_sum.9) | data formatting | bytes 18874368 | tf_op jit(solution)/shard_map/reshape | solution.py:51
  494.8 14.7 %copy.52 = f32[4,2,384,2,384]{2,4,3,1,0:T(8,128)} copy(f32[4,2,384,2,384]{4,3,2,1,0:T(2,128)} %reshape.92) | data formatting | bytes 18874368 | tf_op jit(solution)/shard_map/reshape | solution.py:51
  509.5 9.9 %fusion.1 = bf16[4,2,384,2,384]{4,2,3,1,0:T(8,128)(2,1)} fusion(f32[4,2,384,2,384]{2,4,3,1,0:T(8,128)} %copy.52, f32[4,2,384,2,384]{4,3,2,1,0:T(2,128)} %reshape.92, f32[384]{0:T(512)S(1)} %copy-done.2, f32[4,2,384,2]{2,3,1,0:T(2,128)} %broadcast_subtract_fusion), kind=kLoop, calls=%fused_computation.9 | loop fusion | flops 11796480 | bytes 23619072 | tf_op jit(solution)/shard_map/convert_element_type | solution.py:60
  519.5 9.4 %copy.53 = bf16[4,2,384,2,384]{4,3,2,1,0:T(2,128)(2,1)} copy(bf16[4,2,384,2,384]{4,2,3,1,0:T(8,128)(2,1)} %fusion.1) | data formatting | bytes 9437184 | tf_op jit(solution)/shard_map/convert_element_type | solution.py:60
  528.9 6.7 copy.64
  535.6 11.4 %reshape.94 = bf16[4,768,768]{2,1,0:T(8,128)(2,1)} reshape(bf16[4,2,384,2,384]{4,3,2,1,0:T(2,128)(2,1)} %copy.53) | data formatting | bytes 9437184 | tf_op jit(solution)/shard_map/reshape | solution.py:60
  547.0 5.7 convolution_bitcast_fusion.1
  555.7 13.1 %fusion.3 = f32[288,768,16]{1,2,0:T(8,128)} fusion(f32[288,4,768]{2,0,1:T(8,128)} %convolution_bitcast_fusion.1, s32[4]{0:T(128)S(1)} %copy-done.4), kind=kOutput, calls=%fused_computation.12 | convolution fusion | flops 169869376 | bytes 17694736 | tf_op jit(solution)/shard_map/sk,psx->pkx/dot_general | solution.py:103
  568.8 5.8 convolution_bitcast_fusion
  574.6 22.6 %all-reduce.8.cloned.1.call-done = f32[128,3,384]{2,1,0:T(4,128)} async-done(((f32[128,3,384]{2,1,0:T(4,128)}), f32[128,3,384]{2,1,0:T(4,128)}) %all-reduce.8.cloned.1.call-update) | async-done | bytes 589840
  598.9 15.4 %add_bitcast_fusion = f32[288,16,768]{2,1,0:T(8,128)} fusion(f32[288,768,16]{1,2,0:T(8,128)} %fusion.3, f32[288,4,768]{2,0,1:T(8,128)} %convolution_bitcast_fusion, s32[4]{0:T(128)S(1)} %copy-done.6), kind=kOutput, calls=%fused_computation.6 | convolution fusion | flops 173408320 | bytes 31850512 | tf_op jit(solution)/shard_map/sk,psx->pkx/dot_general | solution.py:105
  614.3 18.3 %copy.56 = f32[288,16,768]{2,0,1:T(8,128)} copy(f32[288,16,768]{2,1,0:T(8,128)} %add_bitcast_fusion) | data formatting | bytes 28311552 | tf_op jit(solution)/shard_map/add | solution.py:103
  642.8 14.0 %all-reduce.3 = f32[8,3,384]{2,1,0:T(4,128)S(1)} all-reduce(f32[8,3,384]{2,1,0:T(4,128)S(1)} %constant_dynamic-slice_fusion.1), channel_id=9, replica_groups=mesh['orow_0'=4,'orow_1'=4,'ocol_0'=4,'ocol_1'=2] {'ocol_0'}, use_global_device_ids=true, to_apply=%region_4.6.clone | all-reduce | flops 9216 | bytes 73728
  656.8 9.2 %all-reduce.4 = f32[2,3,384]{2,1,0:T(4,128)S(1)} all-reduce(f32[2,3,384]{2,1,0:T(4,128)S(1)} %constant_dynamic-slice_fusion), channel_id=10, replica_groups=mesh['orow_0'=4,'orow_1'=4,'ocol_0'=4,'ocol_1'=2] {'ocol_1'}, use_global_device_ids=true, to_apply=%region_5.7.clone | all-reduce | flops 2304 | bytes 18432
  668.5 10.1 %all-gather.1 = f32[8,3,384]{2,1,0:T(4,128)S(1)} all-gather(f32[2,3,384]{2,1,0:T(4,128)S(1)} %all_gather.33), channel_id=3, replica_groups=mesh['orow_0'=4,'orow_1'=4,'ocol_0'=4,'ocol_1'=2] {'ocol_0'}, dimensions={0}, use_global_device_ids=true | all-gather | bytes 46080 | tf_op jit(solution)/shard_map/all_gather | solution.py:32
  678.7 11.2 %all-gather.2 = f32[16,2,3,384]{3,1,2,0:T(2,128)S(1)} all-gather(f32[4,2,3,384]{3,1,2,0:T(2,128)S(1)} %copy.59), channel_id=4, replica_groups=mesh['orow_0'=4,'orow_1'=4,'ocol_0'=4,'ocol_1'=2] {'orow_1'}, dimensions={0}, use_global_device_ids=true | all-gather | bytes 184320 | tf_op jit(solution)/shard_map/all_gather | solution.py:32
  689.9 15.1 %all-gather.3 = f32[16,4,2,3,384]{4,1,3,2,0:T(4,128)S(1)} all-gather(f32[4,4,2,3,384]{4,1,3,2,0:T(4,128)S(1)} %copy.60), channel_id=5, replica_groups=mesh['orow_0'=4,'orow_1'=4,'ocol_0'=4,'ocol_1'=2] {'orow_0'}, dimensions={0}, use_global_device_ids=true | all-gather | bytes 737280 | tf_op jit(solution)/shard_map/all_gather | solution.py:32
  706.5 45.8 %reduce-scatter.4.cloned.1.call-done = f32[288,1,768]{2,0,1:T(8,128)} async-done(((f32[288,16,768]{2,0,1:T(8,128)}), f32[288,1,768]{2,0,1:T(8,128)}) %reduce-scatter.4.cloned.1.call-update) | async-done | bytes 884752
  (72 shorter events, 47.7 us)
Async XLA Ops:
  7.2 4.0 copy-start
  7.2 72.1 %all-gather.7.cloned.1.call-start = ((), (), s32[]{:S(2)}) async-start(), calls=%async_computation.1 | async-start | bytes 7520256 | tf_op jit(solution)/shard_map/all_gather | solution.py:74
  11.0 443.0 %all-gather.9.cloned.1.call-start = ((), (), s32[]{:S(2)}) async-start(), calls=%async_computation.2 | async-start | bytes 84934656 | tf_op jit(solution)/shard_map/all_gather | solution.py:90
  11.8 76.0 %copy-start.3 = (s32[4]{0:T(128)}, s32[4]{0:T(128)S(1)}, u32[]{:S(2)}) copy-start(s32[4]{0:T(128)S(1)} %gather_fusion.1) | copy-start | bytes 52
  13.1 74.7 %copy-start.5 = (s32[4]{0:T(128)}, s32[4]{0:T(128)S(1)}, u32[]{:S(2)}) copy-start(s32[4]{0:T(128)S(1)} %gather_fusion) | copy-start | bytes 52
  120.0 477.2 %all-reduce.8.cloned.1.call-start = ((), (), s32[]{:S(2)}) async-start(), calls=%async_computation.3 | async-start | bytes 1572864
  494.8 14.7 %copy-start.2 = (f32[384]{0:T(512)S(1)}, f32[384]{0:T(512)}, u32[]{:S(2)}) copy-start(f32[384]{0:T(512)} %param.11) | copy-start | bytes 4612
  547.0 8.7 %copy-start.4 = (s32[4]{0:T(128)S(1)}, s32[4]{0:T(128)}, u32[]{:S(2)}) copy-start(s32[4]{0:T(128)} %copy-done.3) | copy-start | bytes 52
  555.6 86.4 %all-reduce.10.cloned.1.call-start = ((), (), s32[]{:S(2)}) async-start(), calls=%async_computation.4 | async-start | bytes 393216
  568.8 30.1 %copy-start.6 = (s32[4]{0:T(128)S(1)}, s32[4]{0:T(128)}, u32[]{:S(2)}) copy-start(s32[4]{0:T(128)} %copy-done.5) | copy-start | bytes 52
  598.8 153.5 %reduce-scatter.4.cloned.1.call-start = ((), (), s32[]{:S(2)}) async-start(), calls=%async_computation.5 | async-start | bytes 15040512
  632.6 0.7 copy-start.9
  632.6 1.2 copy-start.8
  632.6 1.9 copy-start.7
  633.3 121.6 %copy-start.1 = (s32[64,1]{0,1:T(1,128)S(1)}, s32[64,1]{0,1:T(1,128)}, u32[]{:S(2)}) copy-start(s32[64,1]{0,1:T(1,128)} %param.12) | copy-start | bytes 772
Sparse Core Ops, SparseCore 0:
  11.2 68.0 all-gather.6
  120.1 333.9 all-gather.8
  555.7 41.3 all-reduce.7
  599.9 42.0 all-reduce.9
  645.3 106.9 reduce-scatter.3
